TPU v7x, 128 devices: a whole 4x4x4 slice. The times are simulated.
128 devices in a mesh: row: 8 (over x, y_lo), col: 16 (over z, y_hi, core).
Axes of the slice: x: 4, y: 4 (y_hi: 2, y_lo: 2; y = y_hi * 2 + y_lo), z: 4, core: 2. Of those that a mesh axis runs over, the one named last changes fastest.
Arguments:
- amplitudes: float32 [16, 16, 256, 256], P('row', 'col'), may hold values from -6 to 6
- coulomb: bfloat16 [16, 16, 256, 256], P('row'), may hold values from -6 to 6
- inner_list: int32 [16, 16, 8], P('row', 'col'), may hold values from 0 to 15, as said below
- inner_count: int32 [16, 16], P('row', 'col'), may hold values from 4 to 8
- reader_list: int32 [16, 16, 8], P('row'), may hold values from 0 to 15, as said below
- reader_count: int32 [16, 16], P('row'), may hold values from 4 to 8
- virtual_energy: float32 [256], replicated, may hold values from 0.5 to 2.5
- occupied_energy: float32 [16], replicated, may hold values from -1.5 to -0.3
Outputs:
- new_amplitudes: float32 [16, 16, 256, 256], P('row', 'col')
Inputs may be any that keep to these rules, and one draw needn't show every extreme that they name: `inner_list`: for each pair block the 8 entries are distinct orbitals; only the first inner_count of them are used. `reader_list`: for each pair block the 8 entries are distinct orbitals; only the first reader_count of them are used.
All inputs are finite; a program needn't handle non-finite values.
Results may differ from a plain program's by a relative error of at most 0.0015.
Values may be sent and summed in bfloat16 or wider, within the bound.
A program may use at most 64 MiB of HBM per device.

v0:
```python
import jax
import jax.numpy as jnp
from jax import lax
from jax.sharding import PartitionSpec as P

ITERS = 2


damping = 0.5
coupling = 0.03125


def on_device(
    amplitudes,
    coulomb,
    inner_list,
    inner_count,
    reader_list,
    reader_count,
    virtual_energy,
    occupied_energy,
):
    orb_rows = amplitudes.shape[0]
    orb_cols = amplitudes.shape[1]
    slot_count = inner_list.shape[2]
    row_start = lax.axis_index("row") * orb_rows
    col_start = lax.axis_index("col") * orb_cols
    occ_rows = lax.dynamic_slice_in_dim(occupied_energy, row_start, orb_rows, 0)
    occ_cols = lax.dynamic_slice_in_dim(occupied_energy, col_start, orb_cols, 0)
    virt_pair = virtual_energy[:, None] + virtual_energy[None, :]
    denominator = (
        virt_pair[None, None] - occ_rows[:, None, None, None] - occ_cols[None, :, None, None]
    )
    slot_iota = jnp.arange(slot_count, dtype=jnp.int32)
    row_iota = jnp.arange(orb_rows, dtype=jnp.int32)[:, None, None]
    col_iota = jnp.arange(orb_cols, dtype=jnp.int32)[None, :, None]
    inner_mask = (slot_iota < inner_count[..., None]).astype(jnp.bfloat16)[..., None, None]
    own_readers = lax.dynamic_slice_in_dim(reader_list, col_start, orb_cols, 1)
    own_reader_len = lax.dynamic_slice_in_dim(reader_count, col_start, orb_cols, 1)
    reader_mask = (slot_iota < own_reader_len[..., None]).astype(jnp.bfloat16)[..., None, None]
    coulomb_own = lax.dynamic_slice_in_dim(coulomb, col_start, orb_cols, 1).astype(jnp.float32)
    left_inner = coulomb[row_iota, inner_list]
    amp_state = amplitudes
    for sweep_index in range(ITERS):
        amp_half = amp_state.astype(jnp.bfloat16)
        amp_columns = lax.all_gather(amp_half, "row", axis=0, tiled=True)
        right_inner = amp_columns[inner_list, col_iota] * inner_mask
        coupled = jnp.einsum(
            "ijsab,ijsbc->ijac", left_inner, right_inner, preferred_element_type=jnp.float32
        ).astype(jnp.bfloat16)
        coupled_columns = lax.all_gather(coupled, "row", axis=0, tiled=True)
        coupled_rows = lax.all_to_all(
            coupled_columns, "col", split_axis=0, concat_axis=1, tiled=True
        )
        mirror = jnp.transpose(
            lax.dynamic_slice_in_dim(coupled_rows, row_start, orb_rows, 1), (1, 0, 3, 2)
        )
        right_reader = coupled_columns[own_readers, col_iota] * reader_mask
        amp_rows = lax.all_gather(amp_half, "col", axis=1, tiled=True)
        left_reader = amp_rows[row_iota, own_readers]
        quadratic = jnp.einsum(
            "ijsab,ijsbc->ijac", left_reader, right_reader, preferred_element_type=jnp.float32
        )
        residual = (
            coulomb_own
            + coupling * (coupled.astype(jnp.float32) + mirror.astype(jnp.float32))
            + coupling * coupling * quadratic
        )
        amp_state = damping * amp_state - residual / denominator
    return amp_state


def solution(mesh):
    return jax.shard_map(
        on_device,
        mesh=mesh,
        in_specs=(
            P("row", "col", None, None),
            P("row", None, None, None),
            P("row", "col", None),
            P("row", "col"),
            P("row", None, None),
            P("row", None),
            P(),
            P(),
        ),
        out_specs=P("row", "col", None, None),
        check_vma=False,
    )
```

profile of v0, /device:TPU:0, one launch (start us, length us, event | category | flops | bytes accessed | tf_op | source)
XLA Modules:
  0.0 390.8 jit_solution(14267644027346781398)
XLA Ops:
  6.5 1.8 convert_element_type.66
  8.4 0.8 copy.51
  9.2 0.7 broadcast_compare_fusion
  9.9 0.7 broadcast_add_fusion.1
  10.7 0.1 select_reduce_fusion
  11.0 0.9 fusion.67
  12.1 2.9 gather_fusion
  15.0 48.3 %all-gather.9.cloned.1.call-done = bf16[16,1,256,256]{3,2,1,0:T(8,128)(2,1)} async-done(((bf16[2,1,256,256]{3,2,1,0:T(8,128)(2,1)}), bf16[16,1,256,256]{3,2,1,0:T(8,128)(2,1)}) %all-gather.9.cloned.1.call-update) | async-done | bytes 2097168 | tf_op jit(solution)/shard_map/all_gather | solution.py:46
  63.4 3.6 gather_fusion.1
  67.0 3.1 fusion.41
  70.2 0.7 all-gather.11.cloned.1.call-update
  70.9 51.3 %all-gather.17.cloned.1.call-done = bf16[16,256,256]{2,1,0:T(8,128)(2,1)} async-done(((bf16[2,256,256]{2,1,0:T(8,128)(2,1)}), bf16[16,256,256]{2,1,0:T(8,128)(2,1)}) %all-gather.17.cloned.1.call-update) | async-done | bytes 2097168 | tf_op jit(solution)/shard_map/all_gather | solution.py:51
  122.1 5.9 %all-to-all-start = ((bf16[16,1,256,256]{3,2,1,0:T(8,128)(2,1)}), bf16[16,1,256,256]{3,2,1,0:T(8,128)(2,1)}, u32[]{:S(2)}, u32[]{:S(2)}) async-start(bf16[16,1,256,256]{3,2,1,0:T(8,128)(2,1)} %bitcast.127), calls=%async_computation | async-start | bytes 4194304 | tf_op jit(solution)/shard_map/all_to_all | solution.py:52
  128.1 0.7 dynamic_slice.21
  128.9 0.2 fusion.68
  129.5 2.0 gather_fusion.3
  131.5 57.5 %all-gather.11.cloned.1.call-done = bf16[2,16,256,256]{3,2,1,0:T(8,128)(2,1)} async-done(((bf16[2,1,256,256]{3,2,1,0:T(8,128)(2,1)}), bf16[2,16,256,256]{3,2,1,0:T(8,128)(2,1)}) %all-gather.11.cloned.1.call-update) | async-done | bytes 4194320 | tf_op jit(solution)/shard_map/all_gather | solution.py:59
  188.9 4.2 %gather_fusion.2 = bf16[16,256,256]{2,1,0:T(8,128)(2,1)} fusion(bf16[2,16,256,256]{3,2,1,0:T(8,128)(2,1)} %all-gather.11.cloned.1.call-done, s32[16]{0:T(128)S(1)} %reshape.182), kind=kCustom, calls=%fused_computation.2 | custom fusion | bytes 4194432 | tf_op jit(solution)/shard_map/gather | solution.py:60
  193.2 1.0 constant_dynamic-slice_fusion.2
  194.1 0.9 copy.67
  195.0 4.2 %fusion.85 = (bf16[2,1,256,256]{3,2,0,1:T(8,128)(2,1)}, f32[2,1,256,256]{3,2,0,1:T(8,128)}) fusion(f32[]{:T(128)} %bitcast.20, f32[2]{0:T(128)S(1)} %dynamic_slice.20, f32[256,256]{1,0:T(8,128)S(1)} %broadcast_add_fusion, bf16[2,8,256,256]{3,2,1,0:T(8,128)(2,1)} %bitcast.136, bf16[2,8,256,256]{3,2,1,0:T(8,128)(2,1)S(1)} %bitcast.135, ...), kind=kOutput, calls=%fused_computation.88 | convolution fusion | flops 539754496 | bytes 6553648 | tf_op jit(solution)/shard_map/ijsab,ijsbc->ijac/dot_general | solution.py:61
  199.3 49.7 %all-gather.13.cloned.1.call-done = bf16[16,1,256,256]{3,2,1,0:T(8,128)(2,1)} async-done(((bf16[2,1,256,256]{3,2,1,0:T(8,128)(2,1)}), bf16[16,1,256,256]{3,2,1,0:T(8,128)(2,1)}) %all-gather.13.cloned.1.call-update) | async-done | bytes 2097168 | tf_op jit(solution)/shard_map/all_gather | solution.py:46
  248.9 3.6 gather_fusion.4
  252.5 3.1 fusion.38
  255.7 0.5 all-gather.15.cloned.1.call-update
  256.3 51.4 %all-gather.19.cloned.1.call-done = bf16[16,256,256]{2,1,0:T(8,128)(2,1)} async-done(((bf16[2,256,256]{2,1,0:T(8,128)(2,1)}), bf16[16,256,256]{2,1,0:T(8,128)(2,1)}) %all-gather.19.cloned.1.call-update) | async-done | bytes 2097168 | tf_op jit(solution)/shard_map/all_gather | solution.py:51
  307.7 5.9 %all-to-all-start.1 = ((bf16[16,1,256,256]{3,2,1,0:T(8,128)(2,1)}), bf16[16,1,256,256]{3,2,1,0:T(8,128)(2,1)}, u32[]{:S(2)}, u32[]{:S(2)}) async-start(bf16[16,1,256,256]{3,2,1,0:T(8,128)(2,1)} %bitcast.129), calls=%async_computation.1 | async-start | bytes 4194304 | tf_op jit(solution)/shard_map/all_to_all | solution.py:52
  313.6 2.0 gather_fusion.6
  315.6 58.8 %all-gather.15.cloned.1.call-done = bf16[2,16,256,256]{3,2,0,1:T(8,128)(2,1)} async-done(((bf16[2,1,256,256]{3,2,0,1:T(8,128)(2,1)}), bf16[2,16,256,256]{3,2,0,1:T(8,128)(2,1)}) %all-gather.15.cloned.1.call-update) | async-done | bytes 4194320 | tf_op jit(solution)/shard_map/all_gather | solution.py:59
  374.5 4.2 %gather_fusion.5 = bf16[16,256,256]{2,1,0:T(8,128)(2,1)} fusion(bf16[2,16,256,256]{3,2,0,1:T(8,128)(2,1)} %all-gather.15.cloned.1.call-done, s32[16]{0:T(128)S(1)} %reshape.182), kind=kCustom, calls=%fused_computation.5 | custom fusion | bytes 4194432 | tf_op jit(solution)/shard_map/gather | solution.py:60
  378.7 1.0 constant_dynamic-slice_fusion
  379.8 4.1 %fusion.52 = f32[2,1,256,256]{3,2,1,0:T(8,128)} fusion(bf16[2,8,256,256]{3,2,1,0:T(8,128)(2,1)} %bitcast.134, bf16[2,8,256,256]{3,2,1,0:T(8,128)(2,1)S(1)} %bitcast.133, bf16[2,8]{1,0:T(2,128)(2,1)S(1)} %compare_convert_fusion, f32[2,1,256,256]{3,2,0,1:T(8,128)} %get-tuple-element.8, bf16[2,1,256,256]{2,3,0,1:T(8,128)(2,1)S(1)} %copy.68, ...), kind=kOutput, calls=%fused_computation.31 | convolution fusion | flops 539623424 | bytes 6291504 | tf_op jit(solution)/shard_map/ijsab,ijsbc->ijac/dot_general | solution.py:61
  (58 shorter events, 1.4 us)
Async XLA Ops:
  6.5 122.3 %copy-start = (s32[2,16]{1,0:T(2,128)S(1)}, s32[2,16]{1,0:T(2,128)}, u32[]{:S(2)}) copy-start(s32[2,16]{1,0:T(2,128)} %param.13) | copy-start | bytes 388
  6.5 56.8 %all-gather.9.cloned.1.call-start = ((), (), s32[]{:S(2)}) async-start(), calls=%async_computation.2 | async-start | bytes 2359296 | tf_op jit(solution)/shard_map/all_gather | solution.py:46
  8.3 113.8 %all-gather.17.cloned.1.call-start = ((), (), s32[]{:S(2)}) async-start(), calls=%async_computation.6 | async-start | bytes 2359296 | tf_op jit(solution)/shard_map/all_gather | solution.py:51
  12.0 2.9 copy-start.11
  14.9 52.0 %copy-start.3 = (bf16[16,256,256]{2,1,0:T(8,128)(2,1)}, bf16[16,256,256]{2,1,0:T(8,128)(2,1)S(1)}, u32[]{:S(2)}) copy-start(bf16[16,256,256]{2,1,0:T(8,128)(2,1)S(1)} %gather_fusion) | copy-start | bytes 6291460
  70.1 118.8 %all-gather.11.cloned.1.call-start = ((), (), s32[]{:S(2)}) async-start(), calls=%async_computation.3 | async-start | bytes 4456448 | tf_op jit(solution)/shard_map/all_gather | solution.py:59
  122.1 6.0 %copy-start.12 = (f32[16]{0:T(128)S(1)}, f32[16]{0:T(128)}, u32[]{:S(2)}) copy-start(f32[16]{0:T(128)} %param.15) | copy-start | bytes 196
  122.1 7.2 %copy-start.10 = (f32[256]{0:T(256)S(1)}, f32[256]{0:T(256)}, u32[]{:S(2)}) copy-start(f32[256]{0:T(256)} %param.14) | copy-start | bytes 3076
  122.1 7.3 %copy-start.1 = (bf16[16,256,256]{2,1,0:T(8,128)(2,1)S(1)}, bf16[16,256,256]{2,1,0:T(8,128)(2,1)}, u32[]{:S(2)}) copy-start(bf16[16,256,256]{2,1,0:T(8,128)(2,1)} %all-gather.17.cloned.1.call-done) | copy-start | bytes 6291460
  122.1 71.1 %all-to-all-start = ((bf16[16,1,256,256]{3,2,1,0:T(8,128)(2,1)}), bf16[16,1,256,256]{3,2,1,0:T(8,128)(2,1)}, u32[]{:S(2)}, u32[]{:S(2)}) async-start(bf16[16,1,256,256]{3,2,1,0:T(8,128)(2,1)} %bitcast.127), calls=%async_computation | async-start | bytes 4194304 | tf_op jit(solution)/shard_map/all_to_all | solution.py:52
  128.1 120.9 %all-gather.13.cloned.1.call-start = ((), (), s32[]{:S(2)}) async-start(), calls=%async_computation.4 | async-start | bytes 2359296 | tf_op jit(solution)/shard_map/all_gather | solution.py:46
  131.5 63.5 %copy-start.6 = (bf16[16,256,256]{2,1,0:T(8,128)(2,1)S(1)}, bf16[16,256,256]{2,1,0:T(8,128)(2,1)}, u32[]{:S(2)}) copy-start(bf16[16,256,256]{2,1,0:T(8,128)(2,1)} %gather_fusion.3) | copy-start | bytes 6291460
  131.5 63.5 %copy-start.7 = (f32[2,1,256,256]{3,2,1,0:T(8,128)S(1)}, f32[2,1,256,256]{3,2,1,0:T(8,128)}, u32[]{:S(2)}) copy-start(f32[2,1,256,256]{3,2,1,0:T(8,128)} %param.8) | copy-start | bytes 1572868
  131.5 63.5 %copy-start.8 = (bf16[2,256,256]{2,1,0:T(8,128)(2,1)S(1)}, bf16[2,256,256]{2,1,0:T(8,128)(2,1)}, u32[]{:S(2)}) copy-start(bf16[2,256,256]{2,1,0:T(8,128)(2,1)} %fusion.41) | copy-start | bytes 786436
  199.2 53.3 %copy-start.4 = (bf16[16,256,256]{2,1,0:T(8,128)(2,1)S(1)}, bf16[16,256,256]{2,1,0:T(8,128)(2,1)}, u32[]{:S(2)}) copy-start(bf16[16,256,256]{2,1,0:T(8,128)(2,1)} %copy-done.3) | copy-start | bytes 6291460
  199.2 108.5 %all-gather.19.cloned.1.call-start = ((), (), s32[]{:S(2)}) async-start(), calls=%async_computation.7 | async-start | bytes 2359296 | tf_op jit(solution)/shard_map/all_gather | solution.py:51
  255.7 118.8 %all-gather.15.cloned.1.call-start = ((), (), s32[]{:S(2)}) async-start(), calls=%async_computation.5 | async-start | bytes 4456448 | tf_op jit(solution)/shard_map/all_gather | solution.py:59
  307.7 5.9 %copy-start.2 = (bf16[16,256,256]{2,1,0:T(8,128)(2,1)S(1)}, bf16[16,256,256]{2,1,0:T(8,128)(2,1)}, u32[]{:S(2)}) copy-start(bf16[16,256,256]{2,1,0:T(8,128)(2,1)} %all-gather.19.cloned.1.call-done) | copy-start | bytes 6291460
  307.7 71.0 %all-to-all-start.1 = ((bf16[16,1,256,256]{3,2,1,0:T(8,128)(2,1)}), bf16[16,1,256,256]{3,2,1,0:T(8,128)(2,1)}, u32[]{:S(2)}, u32[]{:S(2)}) async-start(bf16[16,1,256,256]{3,2,1,0:T(8,128)(2,1)} %bitcast.129), calls=%async_computation.1 | async-start | bytes 4194304 | tf_op jit(solution)/shard_map/all_to_all | solution.py:52
  315.6 64.2 %copy-start.5 = (bf16[16,256,256]{2,1,0:T(8,128)(2,1)S(1)}, bf16[16,256,256]{2,1,0:T(8,128)(2,1)}, u32[]{:S(2)}) copy-start(bf16[16,256,256]{2,1,0:T(8,128)(2,1)} %gather_fusion.6) | copy-start | bytes 6291460
  315.6 64.2 %copy-start.9 = (bf16[2,256,256]{2,1,0:T(8,128)(2,1)S(1)}, bf16[2,256,256]{2,1,0:T(8,128)(2,1)}, u32[]{:S(2)}) copy-start(bf16[2,256,256]{2,1,0:T(8,128)(2,1)} %fusion.38) | copy-start | bytes 786436
Sparse Core Ops, SparseCore 0:
  9.0 54.3 all-gather.8
  70.2 51.8 all-gather.16
  124.6 64.3 all-gather.10
  199.3 49.5 all-gather.12
  255.8 51.8 all-gather.18
  310.0 64.4 all-gather.14
where the time goes:
time: 393 us; the launch traced here: 391 us
  waiting for transfers between devices  318 us (81%)
  local copies, waits for them, and re-layouts  27.8 us (7%)
  matrix products  14.5 us (4%)
  between operations  13.6 us (3%)
  starting transfers between devices  12.1 us (3%)
  other arithmetic  4.56 us (1%)
    all_gather x2, waiting for transfers between devices, on_device(): amp_rows = lax.all_gather(amp_half, 'col', axis=1, tiled=True)  116 us
    all_gather x2, waiting for transfers between devices, on_device(): coupled_columns = lax.all_gather(coupled, 'row', axis=0, tiled=True)  103 us
    all_gather x2, waiting for transfers between devices, on_device(): amp_columns = lax.all_gather(amp_half, 'row', axis=0, tiled=True)  98 us
    all_to_all x2, starting transfers between devices, on_device(): lax.all_to_all(coupled_columns, 'col', split_axis=0, concat_axis=1, tiled...  11.9 us
    gather x2, local copies, waits for them, and re-layouts, on_device(): left_reader = amp_rows[row_iota, own_readers]  8.44 us
    dot_general x2, matrix products, on_device(): jnp.einsum('ijsab,ijsbc->ijac', left_reader, right_reader, preferred_elem...  8.3 us
  transfers between devices with their start and end apart: 8, of which 6 were waited for; matrix products, arithmetic and copies ran while one was open for 5% of the time, Pallas kernels for 0%

commit v1 on v0

v1 whole, which is shorter than its diff:
```python
import functools

import jax
import jax.numpy as jnp
from jax import lax
from jax.experimental import pallas as pl
from jax.experimental.pallas import tpu as pltpu
from jax.sharding import PartitionSpec as P

ITERS = 2

damping = 0.5
coupling = 0.03125
MESH = pl.DeviceIdType.MESH
F32 = jnp.float32
BF16 = jnp.bfloat16

Y_P, Y_Q, Y_QM, Y_QP, Y_Q2A, Y_Q2B = range(6)
R_Q, R_P, R_QA, R_NA, R_NB, R_PA, R_NRA = range(6, 13)
L_Q, L_P, L_QB, L_NB, L_NA, L_PB, L_NRB = range(13, 20)
COL = 20
N_P, N_Q = 40, 41
ZR_O, ZR_H, ZR_OA, ZR_HA = range(42, 46)
ZL_O, ZL_H, ZL_OB, ZL_HB = range(46, 50)
S_O, S_H, S_M, S_P, S_HM, S_HP, S_2, S_H2 = range(50, 58)
M_0, M_1 = 58, 59
COUNT = 60


def kernel(
    nrow, ncol, slots, V,
    amp_ref, coul_ref, ilist_ref, icnt_ref, rlist_ref, rcnt_ref, virt_ref, occ_ref,
    out_ref,
    amps, coups, rows, coul, mirror, state, acc, base, inv, wlin, wquad,
    send_sem, recv_sem, load_sem,
):
    r = lax.axis_index("row")
    c = lax.axis_index("col")

    def flip(v, bit):
        return v + bit - 2 * bit * lax.rem(v // bit, 2)

    unit = 2 * V // 32
    pcut = 18 * unit
    part_p = pl.ds(0, pcut)
    part_q = pl.ds(pcut, 2 * V - pcut)
    pa, pb = pl.ds(0, pcut // 2), pl.ds(pcut // 2, pcut // 2)
    qhalf = (2 * V - pcut) // 2
    qa, qb = pl.ds(pcut, qhalf), pl.ds(pcut + qhalf, qhalf)
    whole = pl.ds(0, 2 * V)
    half_a, half_b = pl.ds(0, V), pl.ds(V, V)

    ry = flip(r, 1)
    rp, rm, r2 = lax.rem(r + 2, nrow), lax.rem(r + nrow - 2, nrow), lax.rem(r + 4, nrow)
    yp, ym, y2 = flip(rp, 1), flip(rm, 1), flip(r2, 1)
    ch, cs = flip(c, 2), flip(c, 1)
    cp, cm, c2 = lax.rem(c + 4, ncol), lax.rem(c + ncol - 4, ncol), lax.rem(c + 8, ncol)
    hp, hm, h2 = flip(cp, 2), flip(cm, 2), flip(c2, 2)
    to_y, to_right, to_left = (ry, c), (rp, c), (rm, c)
    to_n, to_zr, to_zl, to_s = (ry, ch), (r, cp), (r, cm), (r, cs)
    mrow = c // 2
    slot = lax.rem(c, 2)
    mcol = (2 * r, 2 * r + 1)
    mself = tuple(jnp.logical_and(mrow == r, mcol[a] == c) for a in range(2))

    loads = [
        pltpu.make_async_copy(amp_ref.at[a, 0], state.at[pl.ds(a * V, V)], load_sem.at[a])
        for a in range(2)
    ]
    for a in range(2):
        loads[a].start()
    coul_loads = [
        pltpu.make_async_copy(
            coul_ref.at[a], coul.at[:, pl.ds(a * V, V)], load_sem.at[2 + a]
        )
        for a in range(2)
    ]
    for a in range(2):
        coul_loads[a].start()

    barrier = pltpu.get_barrier_semaphore()
    for dev in (to_y, to_right, to_left, to_n, to_zr, to_zl, to_s):
        pl.semaphore_signal(barrier, inc=1, device_id=dev, device_id_type=MESH)
    for a in range(2):
        @pl.when(jnp.logical_not(mself[a]))
        def _():
            pl.semaphore_signal(barrier, inc=1, device_id=(mrow, mcol[a]), device_id_type=MESH)
    on_diagonal = mrow == r

    @pl.when(on_diagonal)
    def _():
        pl.semaphore_wait(barrier, 8)

    @pl.when(jnp.logical_not(on_diagonal))
    def _():
        pl.semaphore_wait(barrier, 9)

    for a in range(2):
        loads[a].wait()

    def sweep(s, carry):
        def message(src, dst, key, dev, recv_key=None):
            return pltpu.make_async_remote_copy(
                src_ref=src, dst_ref=dst, send_sem=send_sem.at[s, key],
                recv_sem=recv_sem.at[s, key if recv_key is None else recv_key],
                device_id=dev, device_id_type=MESH,
            )

        def send(ref, key, dev):
            message(ref, ref, key, dev).start()

        def arrived(ref, key):
            message(ref, ref, key, to_y).wait_recv()

        def consume(left, weight, right, source, first=False):
            for b in range(2):
                orbital = 2 * source + b
                block = right[s, source, b * V:(b + 1) * V, :]
                for a in range(2):
                    at = slice(a * V, (a + 1) * V)
                    part = jnp.dot(left(orbital, a), block, preferred_element_type=F32)
                    part = part * weight[a, orbital]
                    if first and b == 0:
                        acc[at, :] = part
                    else:
                        acc[at, :] += part

        def open_gather(buf, o):
            own = buf.at[s, r]
            send(own.at[part_p], o + Y_P, to_y)
            send(own.at[part_q], o + R_Q, to_right)
            send(own.at[part_q], o + L_Q, to_left)
            send(own.at[part_q], o + Y_Q, to_y)
            send(own.at[part_p], o + R_P, to_right)
            send(own.at[part_p], o + L_P, to_left)

        def relay_q(buf, o):
            arrived(buf.at[s, rm, part_q], o + R_Q)
            send(buf.at[s, rm, qa], o + R_QA, to_right)
            send(buf.at[s, rm, part_q], o + Y_QM, to_y)
            arrived(buf.at[s, rp, part_q], o + L_Q)
            send(buf.at[s, rp, qb], o + L_QB, to_left)
            send(buf.at[s, rp, part_q], o + Y_QP, to_y)

        def relay_n(buf, o):
            arrived(buf.at[s, ry, part_p], o + Y_P)
            send(buf.at[s, ry, pa], o + R_NA, to_right)
            send(buf.at[s, ry, pb], o + L_NB, to_left)
            send(buf.at[s, ry, pb], o + R_NB, to_right)
            send(buf.at[s, ry, pa], o + L_NA, to_left)

        def relay_p(buf, o):
            arrived(buf.at[s, rm, part_p], o + R_P)
            send(buf.at[s, rm, pa], o + R_PA, to_right)
            arrived(buf.at[s, rp, part_p], o + L_P)
            send(buf.at[s, rp, pb], o + L_PB, to_left)

        def relay_q2(buf, o):
            arrived(buf.at[s, r2, qa], o + R_QA)
            send(buf.at[s, r2, qa], o + Y_Q2A, to_y)
            arrived(buf.at[s, r2, qb], o + L_QB)
            send(buf.at[s, r2, qb], o + Y_Q2B, to_y)

        def relay_nn(buf, o):
            arrived(buf.at[s, ym, pa], o + R_NA)
            send(buf.at[s, ym, pa], o + R_NRA, to_right)
            arrived(buf.at[s, yp, pb], o + L_NB)
            send(buf.at[s, yp, pb], o + L_NRB, to_left)
            arrived(buf.at[s, ym, pb], o + R_NB)
            arrived(buf.at[s, yp, pa], o + L_NA)

        def lin_left(orbital, a):
            return coul[orbital, a * V:(a + 1) * V, :]

        def quad_left(orbital, a):
            return rows[s, orbital, a * V:(a + 1) * V, :]

        start = state[...].astype(BF16)
        amps[s, r] = start
        rows[s, c] = start
        open_gather(amps, 0)
        send(rows.at[s, c], ZR_O, to_zr)
        send(rows.at[s, c], ZL_O, to_zl)
        send(rows.at[s, c], S_O, to_s)

        @pl.when(s == 0)
        def _():
            for weight, entries, count in (
                (wlin, lambda a, t: ilist_ref[a, 0, t], lambda a: icnt_ref[a, 0]),
                (wquad, lambda a, t: rlist_ref[a, c, t], lambda a: rcnt_ref[a, c]),
            ):
                for a in range(2):
                    used = count(a)
                    listed = [jnp.where(t < used, entries(a, t), -1) for t in range(slots)]
                    for orbital in range(ncol):
                        hit = listed[0] == orbital
                        for t in range(1, slots):
                            hit = jnp.logical_or(hit, listed[t] == orbital)
                        weight[a, orbital] = jnp.where(hit, 1.0, 0.0).astype(F32)
            across = jnp.broadcast_to(virt_ref[...], (V, V))
            pair = across + across.T
            for a in range(2):
                inv[a * V:(a + 1) * V, :] = 1.0 / (pair - occ_ref[2 * r + a] - occ_ref[c])
            for a in range(2):
                coul_loads[a].wait()

        consume(lin_left, wlin, amps, r, first=True)
        relay_q(amps, 0)
        relay_n(amps, 0)
        message(amps.at[s, ry, part_p], rows.at[s, c, part_p], N_P, to_n).start()
        relay_p(amps, 0)
        arrived(amps.at[s, ry, part_q], Y_Q)
        message(amps.at[s, ry, part_q], rows.at[s, c, part_q], N_Q, to_n).start()
        arrived(rows.at[s, cm], ZR_O)
        send(rows.at[s, cm, half_a], ZR_OA, to_zr)
        send(rows.at[s, cm], S_M, to_s)
        arrived(rows.at[s, cp], ZL_O)
        send(rows.at[s, cp, half_b], ZL_OB, to_zl)
        send(rows.at[s, cp], S_P, to_s)
        consume(lin_left, wlin, amps, rm)
        relay_q2(amps, 0)
        consume(lin_left, wlin, amps, rp)
        consume(lin_left, wlin, amps, ry)
        relay_nn(amps, 0)
        arrived(rows.at[s, ch, part_p], N_P)
        arrived(rows.at[s, ch, part_q], N_Q)
        send(rows.at[s, ch], ZR_H, to_zr)
        send(rows.at[s, ch], ZL_H, to_zl)
        send(rows.at[s, ch], S_H, to_s)
        arrived(amps.at[s, ym, part_q], Y_QM)
        consume(lin_left, wlin, amps, ym)
        arrived(amps.at[s, yp, part_q], Y_QP)
        consume(lin_left, wlin, amps, yp)
        arrived(amps.at[s, r2, pa], R_PA)
        arrived(amps.at[s, r2, pb], L_PB)
        consume(lin_left, wlin, amps, r2)
        arrived(rows.at[s, c2, half_a], ZR_OA)
        arrived(rows.at[s, c2, half_b], ZL_OB)
        send(rows.at[s, c2], S_2, to_s)
        arrived(amps.at[s, y2, qa], Y_Q2A)
        arrived(amps.at[s, y2, qb], Y_Q2B)
        arrived(amps.at[s, y2, pa], R_NRA)
        arrived(amps.at[s, y2, pb], L_NRB)
        consume(lin_left, wlin, amps, y2)

        coups[s, r] = acc[...].astype(BF16)
        open_gather(coups, COL)
        for a in range(2):
            block = coups.at[s, r, pl.ds(a * V, V)]

            @pl.when(jnp.logical_not(mself[a]))
            def _():
                message(
                    block, mirror.at[s, slot], M_0 + a, (mrow, mcol[a]), M_0 + slot
                ).start()

            @pl.when(mself[a])
            def _():
                mirror[s, a] = coups[s, r, a * V:(a + 1) * V, :]

        for a in range(2):
            at = slice(a * V, (a + 1) * V)
            linear = coul[c, at, :].astype(F32) + coupling * coups[s, r, at, :].astype(F32)
            base[at, :] = damping * state[at, :] - linear * inv[at, :]
        relay_q(coups, COL)
        relay_n(coups, COL)
        arrived(rows.at[s, hm], ZR_H)
        send(rows.at[s, hm, half_a], ZR_HA, to_zr)
        send(rows.at[s, hm], S_HM, to_s)
        arrived(rows.at[s, hp], ZL_H)
        send(rows.at[s, hp, half_b], ZL_HB, to_zl)
        send(rows.at[s, hp], S_HP, to_s)
        relay_p(coups, COL)
        relay_q2(coups, COL)
        arrived(coups.at[s, ry, part_q], COL + Y_Q)
        arrived(rows.at[s, h2, half_a], ZR_HA)
        arrived(rows.at[s, h2, half_b], ZL_HB)
        send(rows.at[s, h2], S_H2, to_s)
        for own, key in (
            (c, S_O), (ch, S_H), (cm, S_M), (cp, S_P),
            (hm, S_HM), (hp, S_HP), (c2, S_2), (h2, S_H2),
        ):
            arrived(rows.at[s, flip(own, 1)], key)
        consume(quad_left, wquad, coups, r, first=True)
        consume(quad_left, wquad, coups, rm)
        relay_nn(coups, COL)
        consume(quad_left, wquad, coups, rp)
        consume(quad_left, wquad, coups, ry)
        arrived(coups.at[s, ym, part_q], COL + Y_QM)
        consume(quad_left, wquad, coups, ym)
        arrived(coups.at[s, yp, part_q], COL + Y_QP)
        consume(quad_left, wquad, coups, yp)
        arrived(coups.at[s, r2, pa], COL + R_PA)
        arrived(coups.at[s, r2, pb], COL + L_PB)
        consume(quad_left, wquad, coups, r2)
        for a in range(2):
            @pl.when(jnp.logical_not(mself[a]))
            def _():
                arrived(mirror.at[s, a], M_0 + a)

            at = slice(a * V, (a + 1) * V)
            flipped = mirror[s, a].astype(F32).T
            base[at, :] -= coupling * flipped * inv[at, :]
        arrived(coups.at[s, y2, qa], COL + Y_Q2A)
        arrived(coups.at[s, y2, qb], COL + Y_Q2B)
        arrived(coups.at[s, y2, pa], COL + R_NRA)
        arrived(coups.at[s, y2, pb], COL + L_NRB)
        consume(quad_left, wquad, coups, y2)
        state[...] = base[...] - (coupling * coupling) * acc[...] * inv[...]
        return carry

    lax.fori_loop(0, ITERS, sweep, 0)

    stores = [
        pltpu.make_async_copy(state.at[pl.ds(a * V, V)], out_ref.at[a, 0], load_sem.at[a])
        for a in range(2)
    ]
    for a in range(2):
        stores[a].start()
    sizes = {}
    for o in (0, COL):
        for keys, ref in (
            ((Y_P, R_P, L_P), amps.at[0, r, part_p]),
            ((Y_Q, Y_QM, Y_QP, R_Q, L_Q), amps.at[0, r, part_q]),
            ((Y_Q2A, Y_Q2B, R_QA, L_QB), amps.at[0, r, qa]),
            ((R_NA, R_NB, R_PA, R_NRA, L_NB, L_NA, L_PB, L_NRB), amps.at[0, r, pa]),
        ):
            for key in keys:
                sizes[o + key] = ref
    sizes[N_P], sizes[N_Q] = amps.at[0, r, part_p], amps.at[0, r, part_q]
    for key in (ZR_O, ZR_H, ZL_O, ZL_H, *range(S_O, S_H2 + 1)):
        sizes[key] = rows.at[0, c]
    for key in (ZR_OA, ZR_HA, ZL_OB, ZL_HB):
        sizes[key] = rows.at[0, c, half_a]

    def drain(s, carry):
        def sent(ref, key):
            pltpu.make_async_remote_copy(
                src_ref=ref, dst_ref=ref, send_sem=send_sem.at[s, key],
                recv_sem=recv_sem.at[s, key], device_id=to_y, device_id_type=MESH,
            ).wait_send()

        for key, ref in sizes.items():
            sent(ref, key)
        for a in range(2):
            @pl.when(jnp.logical_not(mself[a]))
            def _():
                sent(mirror.at[0, a], M_0 + a)
        return carry

    lax.fori_loop(0, ITERS, drain, 0)
    for a in range(2):
        stores[a].wait()


def on_device(
    amplitudes,
    coulomb,
    inner_list,
    inner_count,
    reader_list,
    reader_count,
    virtual_energy,
    occupied_energy,
    *,
    nrow,
    ncol,
):
    V = amplitudes.shape[2]
    slots = inner_list.shape[2]
    hbm = pl.BlockSpec(memory_space=pl.ANY)
    smem = pl.BlockSpec(memory_space=pltpu.SMEM)
    vmem = pl.BlockSpec(memory_space=pltpu.VMEM)
    return pl.pallas_call(
        functools.partial(kernel, nrow, ncol, slots, V),
        out_shape=jax.ShapeDtypeStruct(amplitudes.shape, F32),
        in_specs=[hbm, hbm, smem, smem, smem, smem, vmem, smem],
        out_specs=hbm,
        scratch_shapes=[
            pltpu.VMEM((ITERS, nrow, 2 * V, V), BF16),
            pltpu.VMEM((ITERS, nrow, 2 * V, V), BF16),
            pltpu.VMEM((ITERS, ncol, 2 * V, V), BF16),
            pltpu.VMEM((ncol, 2 * V, V), BF16),
            pltpu.VMEM((ITERS, 2, V, V), BF16),
            pltpu.VMEM((2 * V, V), F32),
            pltpu.VMEM((2 * V, V), F32),
            pltpu.VMEM((2 * V, V), F32),
            pltpu.VMEM((2 * V, V), F32),
            pltpu.SMEM((2, ncol), F32),
            pltpu.SMEM((2, ncol), F32),
            pltpu.SemaphoreType.DMA((ITERS, COUNT)),
            pltpu.SemaphoreType.DMA((ITERS, COUNT)),
            pltpu.SemaphoreType.DMA((4,)),
        ],
        compiler_params=pltpu.CompilerParams(
            collective_id=0, has_side_effects=True, vmem_limit_bytes=48 * 1024 * 1024
        ),
        name="sweeps",
    )(
        amplitudes,
        coulomb,
        inner_list,
        inner_count,
        reader_list,
        reader_count,
        virtual_energy.reshape(1, V),
        occupied_energy,
    )


def solution(mesh):
    return jax.shard_map(
        functools.partial(on_device, nrow=mesh.shape["row"], ncol=mesh.shape["col"]),
        mesh=mesh,
        in_specs=(
            P("row", "col", None, None),
            P("row", None, None, None),
            P("row", "col", None),
            P("row", "col"),
            P("row", None, None),
            P("row", None),
            P(),
            P(),
        ),
        out_specs=P("row", "col", None, None),
        check_vma=False,
    )
```

time: 393 us -> 109 us (0.28)
  waiting for transfers between devices: 318 us -> 0 us
  Pallas kernels: 0 us -> 100 us
  local copies, waits for them, and re-layouts: 27.8 us -> 8.23 us
  matrix products: 14.5 us -> 0 us
  between operations: 13.6 us -> 0.02 us
  starting transfers between devices: 12.1 us -> 0 us
  other arithmetic: 4.56 us -> 0 us
    all_gather x6 -> x0, waiting for transfers between devices: 317 us -> none  [the longest x2 116 us: on_device(): amp_rows = lax.all_gather(amp_half, 'col', axis=1, tiled=True)]
    pallas_call x0 -> x1, Pallas kernels: none -> 100 us  [on_device(): pl.pallas_call(functools.partial(kernel, nrow, ncol, slots, V), out_shape...]
    gather x7 -> x0, local copies, waits for them, and re-layouts: 22.6 us -> none  [the longest x2 8.44 us: on_device(): left_reader = amp_rows[row_iota, own_readers]]
    dot_general x4 -> x0, matrix products: 14.5 us -> none  [the longest x2 8.3 us: on_device(): jnp.einsum('ijsab,ijsbc->ijac', left_reader, right_reader, preferred_elem...]
    all_to_all x2 -> x0, starting transfers between devices: 11.9 us -> none  [on_device(): lax.all_to_all(coupled_columns, 'col', split_axis=0, concat_axis=1, tiled...]
    unnamed x29 -> x15, local copies, waits for them, and re-layouts: 1.81 us -> 8.23 us
  transfers between devices with their start and end apart: 8 -> 0, of which waited for: 6 -> 0; matrix products, arithmetic and copies ran while one was open for 5% -> 0% of each run, Pallas kernels for 0% -> 0%
where the time goes in v1:
time: 109 us
  Pallas kernels  100 us (92%)
  local copies, waits for them, and re-layouts  8.23 us (8%)
    pallas_call x1, Pallas kernels, on_device(): pl.pallas_call(functools.partial(kernel, nrow, ncol, slots, V), out_shape...  100 us
    unnamed x15, local copies, waits for them, and re-layouts  8.23 us

profile of v1, /device:TPU:0, one launch (start us, length us, event | category | flops | bytes accessed | tf_op | source)
XLA Modules:
  0.0 108.6 jit_solution(16923997822592017885)
XLA Ops:
  0.0 0.7 copy.9.icnt_ref
  0.7 0.8 copy.10.rlist_ref
  1.5 0.0 copy-start
  1.5 2.2 %copy-done = bf16[2,16,256,256]{3,2,1,0:T(8,128)(2,1)S(1)} copy-done((bf16[2,16,256,256]{3,2,1,0:T(8,128)(2,1)S(1)}, bf16[2,16,256,256]{3,2,1,0:T(8,128)(2,1)}, u32[]{:S(2)}) %copy-start) | copy-done | bytes 4194328
  3.7 0.0 copy-start.1
  3.7 1.0 copy-done.1
  4.7 0.0 copy-start.2
  4.7 0.7 copy-done.2
  5.4 0.0 copy-start.3
  5.4 0.7 copy-done.3
  6.1 0.0 copy-start.4
  6.1 0.7 copy-done.4
  6.8 0.0 copy-start.5
  6.8 0.7 copy-done.5
  7.4 100.3 %sweeps.1 = f32[2,1,256,256]{3,2,1,0:T(8,128)S(1)} custom-call(f32[2,1,256,256]{3,2,1,0:T(8,128)S(1)} %copy-done.1, bf16[2,16,256,256]{3,2,1,0:T(8,128)(2,1)S(1)} %copy-done, s32[2,1,8]{2,1,0:T(1,128)S(1)} %copy-done.2, s32[2,1]{1,0:T(2,128)S(1)} %copy.9.icnt_ref, s32[2,16,8]{2,1,0:T(8,128)S(1)} %copy.10.rlist_ref, s32[2,16]{1,0:T(2,128)S(1)} %copy-done.3, ...), custom_call_target="tpu_custom_call" | custom-call | tf_op jit(solution)/shard_map/sweeps/pallas_call | solution.py:374
  107.8 0.8 copy.12
Async XLA Ops:
  1.5 2.2 %copy-start = (bf16[2,16,256,256]{3,2,1,0:T(8,128)(2,1)S(1)}, bf16[2,16,256,256]{3,2,1,0:T(8,128)(2,1)}, u32[]{:S(2)}) copy-start(bf16[2,16,256,256]{3,2,1,0:T(8,128)(2,1)} %coul_ref.1) | copy-start | bytes 12582916
  3.7 1.0 copy-start.1
  4.7 0.7 copy-start.2
  5.4 0.7 copy-start.3
  6.1 0.7 copy-start.4
  6.8 0.7 copy-start.5

commit v2 on v1

v2 whole, which is shorter than its diff:
```python
import functools

import jax
import jax.numpy as jnp
from jax import lax
from jax.experimental import pallas as pl
from jax.experimental.pallas import tpu as pltpu
from jax.sharding import PartitionSpec as P

ITERS = 2

damping = 0.5
coupling = 0.03125
MESH = pl.DeviceIdType.MESH
F32 = jnp.float32
BF16 = jnp.bfloat16

Y_P, Y_Q, Y_QM, Y_QP, Y_Q2A, Y_Q2B = range(6)
R_Q, R_P, R_QA, R_NA, R_NB, R_PA, R_NRA = range(6, 13)
L_Q, L_P, L_QB, L_NB, L_NA, L_PB, L_NRB = range(13, 20)
COL = 20
N_P, N_Q = 40, 41
ZR_O, ZR_H, ZR_OA, ZR_HA = range(42, 46)
ZL_O, ZL_H, ZL_OB, ZL_HB = range(46, 50)
S_O, S_H, S_M, S_P, S_HM, S_HP, S_2, S_H2 = range(50, 58)
M_0, M_1, X_0, X_1 = range(58, 62)
COUNT = 62
LINEAR_CUT, COUPLED_CUT = 18, 16


def kernel(
    nrow, ncol, slots, V,
    amp_ref, coul_ref, ilist_ref, icnt_ref, rlist_ref, rcnt_ref, virt_ref, occ_ref,
    out_ref,
    amps, coups, rows, coul, mirror, transit, state, acc, base, inv, wlin, wquad,
    ilist, icnt, rlist, rcnt, virt, occ,
    send_sem, recv_sem, load_sem,
):
    r = lax.axis_index("row")
    c = lax.axis_index("col")

    def flip(v, bit):
        return v + bit - 2 * bit * lax.rem(v // bit, 2)

    unit = 2 * V // 32

    def cut(parts):
        first, rest = parts * unit, (32 - parts) * unit
        return dict(
            p=pl.ds(0, first), pa=pl.ds(0, first // 2), pb=pl.ds(first // 2, first // 2),
            q=pl.ds(first, rest), qa=pl.ds(first, rest // 2),
            qb=pl.ds(first + rest // 2, rest // 2),
        )

    lin, quad = cut(LINEAR_CUT), cut(COUPLED_CUT)
    cuts = {0: lin, COL: quad}
    half_a, half_b = pl.ds(0, V), pl.ds(V, V)

    ry = flip(r, 1)
    rp, rm, r2 = lax.rem(r + 2, nrow), lax.rem(r + nrow - 2, nrow), lax.rem(r + 4, nrow)
    yp, ym, y2 = flip(rp, 1), flip(rm, 1), flip(r2, 1)
    ch, cs = flip(c, 2), flip(c, 1)
    cp, cm, c2 = lax.rem(c + 4, ncol), lax.rem(c + ncol - 4, ncol), lax.rem(c + 8, ncol)
    hp, hm, h2 = flip(cp, 2), flip(cm, 2), flip(c2, 2)
    to_y, to_right, to_left = (ry, c), (rp, c), (rm, c)
    to_n, to_zr, to_zl, to_s = (ry, ch), (r, cp), (r, cm), (r, cs)
    nx = nrow // 2
    x, lo = r // 2, lax.rem(r, 2)
    z, hi, core = c // 4, lax.rem(c // 2, 2), lax.rem(c, 2)
    ahead = lax.rem(z - x + nx, nx)

    def place(px, pz, plo, phi, pcore):
        return (
            2 * lax.rem(px + nx, nx) + plo, 4 * lax.rem(pz + nx, nx) + 2 * phi + pcore
        )

    step = 2 - ahead
    diagonal = ahead == 0
    opposite = ahead == 2
    beside = jnp.logical_or(ahead == 1, ahead == 3)
    mself = tuple(
        jnp.logical_and(diagonal, jnp.logical_and(lo == hi, core == a)) for a in range(2)
    )
    mout = tuple(jnp.logical_and(diagonal, jnp.logical_not(mself[a])) for a in range(2))

    loads = [
        pltpu.make_async_copy(amp_ref.at[a, 0], state.at[pl.ds(a * V, V)], load_sem.at[a])
        for a in range(2)
    ]
    for a in range(2):
        loads[a].start()
    coul_loads = [
        pltpu.make_async_copy(
            coul_ref.at[a], coul.at[:, pl.ds(a * V, V)], load_sem.at[2 + a]
        )
        for a in range(2)
    ]
    for a in range(2):
        coul_loads[a].start()
    small_loads = [
        pltpu.make_async_copy(src, dst, load_sem.at[4 + at])
        for at, (src, dst) in enumerate((
            (ilist_ref, ilist), (icnt_ref, icnt), (rlist_ref, rlist), (rcnt_ref, rcnt),
            (virt_ref, virt), (occ_ref, occ),
        ))
    ]
    for load in small_loads:
        load.start()

    barrier = pltpu.get_barrier_semaphore()
    for dev in (to_y, to_right, to_left, to_n, to_zr, to_zl, to_s):
        pl.semaphore_signal(barrier, inc=1, device_id=dev, device_id_type=MESH)

    def greet(condition, *devices):
        @pl.when(condition)
        def _():
            for dev in devices:
                pl.semaphore_signal(barrier, inc=1, device_id=dev, device_id_type=MESH)

    greet(diagonal, place(x, z + 1, hi, lo, core), place(x, z - 1, hi, lo, core))
    for a in range(2):
        greet(mout[a], place(x, z, hi, lo, a))
        greet(jnp.logical_and(beside, core == 0), place(z, x, hi, lo, a))
        greet(jnp.logical_and(beside, core == 1), place(z, z, lo, hi, a))
        greet(jnp.logical_and(opposite, core == 0), place(x - 1, z, lo, hi, a))
        greet(jnp.logical_and(opposite, core == 1), place(x + 1, z, lo, hi, a))
    greet(beside, place(x - step, z, lo, hi, core), place(x, z + 2, hi, lo, core))
    for condition, count in (
        (jnp.logical_or(beside, jnp.logical_and(diagonal, lo != hi)), 11),
        (jnp.logical_and(diagonal, lo == hi), 10),
        (opposite, 9),
    ):
        @pl.when(condition)
        def _():
            pl.semaphore_wait(barrier, count)

    for a in range(2):
        loads[a].wait()

    def sweep(s, carry):
        def message(src, dst, key, dev, recv_key=None):
            return pltpu.make_async_remote_copy(
                src_ref=src, dst_ref=dst, send_sem=send_sem.at[s, key],
                recv_sem=recv_sem.at[s, key if recv_key is None else recv_key],
                device_id=dev, device_id_type=MESH,
            )

        def send(ref, key, dev):
            message(ref, ref, key, dev).start()

        def arrived(ref, key):
            message(ref, ref, key, to_y).wait_recv()

        def consume(left, weight, right, source, first=False):
            for b in range(2):
                orbital = 2 * source + b
                block = right[s, source, b * V:(b + 1) * V, :]
                for a in range(2):
                    at = slice(a * V, (a + 1) * V)
                    part = jnp.dot(left(orbital, a), block, preferred_element_type=F32)
                    part = part * weight[a, orbital]
                    if first and b == 0:
                        acc[at, :] = part
                    else:
                        acc[at, :] += part

        def open_gather(buf, o):
            k = cuts[o]
            own = buf.at[s, r]
            send(own.at[k["p"]], o + Y_P, to_y)
            send(own.at[k["q"]], o + R_Q, to_right)
            send(own.at[k["q"]], o + L_Q, to_left)
            send(own.at[k["q"]], o + Y_Q, to_y)
            send(own.at[k["p"]], o + R_P, to_right)
            send(own.at[k["p"]], o + L_P, to_left)

        def relay_q(buf, o):
            k = cuts[o]
            arrived(buf.at[s, rm, k["q"]], o + R_Q)
            send(buf.at[s, rm, k["qa"]], o + R_QA, to_right)
            send(buf.at[s, rm, k["q"]], o + Y_QM, to_y)
            arrived(buf.at[s, rp, k["q"]], o + L_Q)
            send(buf.at[s, rp, k["qb"]], o + L_QB, to_left)
            send(buf.at[s, rp, k["q"]], o + Y_QP, to_y)

        def relay_n(buf, o):
            k = cuts[o]
            arrived(buf.at[s, ry, k["p"]], o + Y_P)
            send(buf.at[s, ry, k["pa"]], o + R_NA, to_right)
            send(buf.at[s, ry, k["pb"]], o + L_NB, to_left)
            send(buf.at[s, ry, k["pb"]], o + R_NB, to_right)
            send(buf.at[s, ry, k["pa"]], o + L_NA, to_left)

        def relay_p(buf, o):
            k = cuts[o]
            arrived(buf.at[s, rm, k["p"]], o + R_P)
            send(buf.at[s, rm, k["pa"]], o + R_PA, to_right)
            arrived(buf.at[s, rp, k["p"]], o + L_P)
            send(buf.at[s, rp, k["pb"]], o + L_PB, to_left)

        def relay_q2(buf, o):
            k = cuts[o]
            arrived(buf.at[s, r2, k["qa"]], o + R_QA)
            send(buf.at[s, r2, k["qa"]], o + Y_Q2A, to_y)
            arrived(buf.at[s, r2, k["qb"]], o + L_QB)
            send(buf.at[s, r2, k["qb"]], o + Y_Q2B, to_y)

        def relay_nn(buf, o):
            k = cuts[o]
            arrived(buf.at[s, ym, k["pa"]], o + R_NA)
            send(buf.at[s, ym, k["pa"]], o + R_NRA, to_right)
            arrived(buf.at[s, yp, k["pb"]], o + L_NB)
            send(buf.at[s, yp, k["pb"]], o + L_NRB, to_left)
            arrived(buf.at[s, ym, k["pb"]], o + R_NB)
            arrived(buf.at[s, yp, k["pa"]], o + L_NA)

        def lin_left(orbital, a):
            return coul[orbital, a * V:(a + 1) * V, :]

        def quad_left(orbital, a):
            return rows[s, orbital, a * V:(a + 1) * V, :]

        start = state[...].astype(BF16)
        amps[s, r] = start
        rows[s, c] = start
        open_gather(amps, 0)
        send(rows.at[s, c], ZR_O, to_zr)
        send(rows.at[s, c], ZL_O, to_zl)
        send(rows.at[s, c], S_O, to_s)

        @pl.when(s == 0)
        def _():
            for load in small_loads:
                load.wait()
            for weight, entries, count in (
                (wlin, lambda a, t: ilist[a, 0, t], lambda a: icnt[0, a]),
                (wquad, lambda a, t: rlist[a, t, c], lambda a: rcnt[a, c]),
            ):
                for a in range(2):
                    used = count(a)
                    listed = [jnp.where(t < used, entries(a, t), -1) for t in range(slots)]
                    for orbital in range(ncol):
                        hit = listed[0] == orbital
                        for t in range(1, slots):
                            hit = jnp.logical_or(hit, listed[t] == orbital)
                        weight[a, orbital] = jnp.where(hit, 1.0, 0.0).astype(F32)
            across = jnp.broadcast_to(virt[...], (V, V))
            pair = across + across.T
            for a in range(2):
                inv[a * V:(a + 1) * V, :] = 1.0 / (pair - occ[2 * r + a] - occ[c])
            for a in range(2):
                coul_loads[a].wait()

        consume(lin_left, wlin, amps, r, first=True)
        relay_q(amps, 0)
        relay_n(amps, 0)
        message(amps.at[s, ry, lin["p"]], rows.at[s, c, lin["p"]], N_P, to_n).start()
        relay_p(amps, 0)
        arrived(amps.at[s, ry, lin["q"]], Y_Q)
        message(amps.at[s, ry, lin["q"]], rows.at[s, c, lin["q"]], N_Q, to_n).start()
        arrived(rows.at[s, cm], ZR_O)
        send(rows.at[s, cm, half_a], ZR_OA, to_zr)
        send(rows.at[s, cm], S_M, to_s)
        arrived(rows.at[s, cp], ZL_O)
        send(rows.at[s, cp, half_b], ZL_OB, to_zl)
        send(rows.at[s, cp], S_P, to_s)
        consume(lin_left, wlin, amps, rm)
        relay_q2(amps, 0)
        consume(lin_left, wlin, amps, rp)
        consume(lin_left, wlin, amps, ry)
        relay_nn(amps, 0)
        arrived(rows.at[s, ch, lin["p"]], N_P)
        arrived(rows.at[s, ch, lin["q"]], N_Q)
        send(rows.at[s, ch], ZR_H, to_zr)
        send(rows.at[s, ch], ZL_H, to_zl)
        send(rows.at[s, ch], S_H, to_s)
        arrived(amps.at[s, ym, lin["q"]], Y_QM)
        consume(lin_left, wlin, amps, ym)
        arrived(amps.at[s, yp, lin["q"]], Y_QP)
        consume(lin_left, wlin, amps, yp)
        arrived(amps.at[s, r2, lin["pa"]], R_PA)
        arrived(amps.at[s, r2, lin["pb"]], L_PB)
        consume(lin_left, wlin, amps, r2)
        arrived(rows.at[s, c2, half_a], ZR_OA)
        arrived(rows.at[s, c2, half_b], ZL_OB)
        send(rows.at[s, c2], S_2, to_s)
        arrived(amps.at[s, y2, lin["qa"]], Y_Q2A)
        arrived(amps.at[s, y2, lin["qb"]], Y_Q2B)
        arrived(amps.at[s, y2, lin["pa"]], R_NRA)
        arrived(amps.at[s, y2, lin["pb"]], L_NRB)
        consume(lin_left, wlin, amps, y2)

        coups[s, r] = acc[...].astype(BF16)
        block = [coups.at[s, r, half_a], coups.at[s, r, half_b]]
        final = (mirror.at[s, core], M_0 + core)

        def forward(src, key, target, dev):
            message(src, target[0], key, dev, target[1]).start()

        @pl.when(opposite)
        def _():
            first = (transit.at[s, 0], X_0)
            forward(block[0], M_0, first, place(x + 1, z, lo, hi, core))
            forward(block[1], M_1, first, place(x - 1, z, lo, hi, core))

        open_gather(coups, COL)

        @pl.when(beside)
        def _():
            crossing = ahead // 2
            forward(
                block[1], M_1, (transit.at[s, crossing], X_0 + crossing),
                place(x, x, hi, lo, core),
            )
            forward(block[0], M_0, final, place(z, x, hi, lo, 0))

        for a in range(2):
            @pl.when(mout[a])
            def _():
                forward(block[a], M_0 + a, final, place(x, z, hi, lo, a))

            @pl.when(mself[a])
            def _():
                mirror[s, a] = coups[s, r, a * V:(a + 1) * V, :]

        for a in range(2):
            at = slice(a * V, (a + 1) * V)
            linear = coul[c, at, :].astype(F32) + coupling * coups[s, r, at, :].astype(F32)
            base[at, :] = damping * state[at, :] - linear * inv[at, :]
        relay_q(coups, COL)
        relay_n(coups, COL)

        @pl.when(diagonal)
        def _():
            for at, px in ((0, x + 1), (1, x - 1)):
                arrived(transit.at[s, at], X_0 + at)
                forward(transit.at[s, at], X_0 + at, final, place(px, z, lo, hi, 1))

        @pl.when(beside)
        def _():
            arrived(transit.at[s, 0], X_0)
            forward(
                transit.at[s, 0], X_0, (transit.at[s, 1], X_1), place(x, z + 2, hi, lo, core)
            )

        arrived(rows.at[s, hm], ZR_H)
        send(rows.at[s, hm, half_a], ZR_HA, to_zr)
        send(rows.at[s, hm], S_HM, to_s)
        arrived(rows.at[s, hp], ZL_H)
        send(rows.at[s, hp, half_b], ZL_HB, to_zl)
        send(rows.at[s, hp], S_HP, to_s)
        relay_p(coups, COL)
        relay_q2(coups, COL)

        @pl.when(beside)
        def _():
            arrived(transit.at[s, 1], X_1)
            forward(transit.at[s, 1], X_1, final, place(x - step, z, lo, hi, ahead % 3))

        arrived(coups.at[s, ry, quad["q"]], COL + Y_Q)
        arrived(rows.at[s, h2, half_a], ZR_HA)
        arrived(rows.at[s, h2, half_b], ZL_HB)
        send(rows.at[s, h2], S_H2, to_s)
        for own, key in (
            (c, S_O), (ch, S_H), (cm, S_M), (cp, S_P),
            (hm, S_HM), (hp, S_HP), (c2, S_2), (h2, S_H2),
        ):
            arrived(rows.at[s, flip(own, 1)], key)
        consume(quad_left, wquad, coups, r, first=True)
        consume(quad_left, wquad, coups, rm)
        relay_nn(coups, COL)
        consume(quad_left, wquad, coups, rp)
        consume(quad_left, wquad, coups, ry)
        arrived(coups.at[s, ym, quad["q"]], COL + Y_QM)
        consume(quad_left, wquad, coups, ym)
        arrived(coups.at[s, yp, quad["q"]], COL + Y_QP)
        consume(quad_left, wquad, coups, yp)
        arrived(coups.at[s, r2, quad["pa"]], COL + R_PA)
        arrived(coups.at[s, r2, quad["pb"]], COL + L_PB)
        consume(quad_left, wquad, coups, r2)
        for a in range(2):
            @pl.when(jnp.logical_not(mself[a]))
            def _():
                arrived(mirror.at[s, a], M_0 + a)

            at = slice(a * V, (a + 1) * V)
            flipped = mirror[s, a].astype(F32).T
            base[at, :] -= coupling * flipped * inv[at, :]
        arrived(coups.at[s, y2, quad["qa"]], COL + Y_Q2A)
        arrived(coups.at[s, y2, quad["qb"]], COL + Y_Q2B)
        arrived(coups.at[s, y2, quad["pa"]], COL + R_NRA)
        arrived(coups.at[s, y2, quad["pb"]], COL + L_NRB)
        consume(quad_left, wquad, coups, y2)
        state[...] = base[...] - (coupling * coupling) * acc[...] * inv[...]
        return carry

    lax.fori_loop(0, ITERS, sweep, 0)
    for a in range(2):
        out_ref[a, 0] = state[a * V:(a + 1) * V, :]
    sizes = {}
    for o, k in cuts.items():
        for keys, part in (
            ((Y_P, R_P, L_P), "p"),
            ((Y_Q, Y_QM, Y_QP, R_Q, L_Q), "q"),
            ((Y_Q2A, Y_Q2B, R_QA, L_QB), "qa"),
            ((R_NA, R_NB, R_PA, R_NRA, L_NB, L_NA, L_PB, L_NRB), "pa"),
        ):
            for key in keys:
                sizes[o + key] = amps.at[0, r, k[part]]
    sizes[N_P], sizes[N_Q] = amps.at[0, r, lin["p"]], amps.at[0, r, lin["q"]]
    for key in (ZR_O, ZR_H, ZL_O, ZL_H, *range(S_O, S_H2 + 1)):
        sizes[key] = rows.at[0, c]
    for key in (ZR_OA, ZR_HA, ZL_OB, ZL_HB):
        sizes[key] = rows.at[0, c, half_a]

    def drain(s, carry):
        def sent(ref, key):
            pltpu.make_async_remote_copy(
                src_ref=ref, dst_ref=ref, send_sem=send_sem.at[s, key],
                recv_sem=recv_sem.at[s, key], device_id=to_y, device_id_type=MESH,
            ).wait_send()

        for key, ref in sizes.items():
            sent(ref, key)
        for a in range(2):
            @pl.when(jnp.logical_not(mself[a]))
            def _():
                sent(mirror.at[0, a], M_0 + a)

        @pl.when(jnp.logical_not(opposite))
        def _():
            for a in range(2):
                sent(transit.at[0, a], X_0 + a)

        return carry

    lax.fori_loop(0, ITERS, drain, 0)


def on_device(
    amplitudes,
    coulomb,
    inner_list,
    inner_count,
    reader_list,
    reader_count,
    virtual_energy,
    occupied_energy,
    *,
    nrow,
    ncol,
):
    V = amplitudes.shape[2]
    slots = inner_list.shape[2]
    hbm = pl.BlockSpec(memory_space=pltpu.HBM)
    vmem = pl.BlockSpec(memory_space=pltpu.VMEM)
    return pl.pallas_call(
        functools.partial(kernel, nrow, ncol, slots, V),
        out_shape=jax.ShapeDtypeStruct(amplitudes.shape, F32),
        in_specs=[hbm] * 8,
        out_specs=vmem,
        scratch_shapes=[
            pltpu.VMEM((ITERS, nrow, 2 * V, V), BF16),
            pltpu.VMEM((ITERS, nrow, 2 * V, V), BF16),
            pltpu.VMEM((ITERS, ncol, 2 * V, V), BF16),
            pltpu.VMEM((ncol, 2 * V, V), BF16),
            pltpu.VMEM((ITERS, 2, V, V), BF16),
            pltpu.VMEM((ITERS, 2, V, V), BF16),
            pltpu.VMEM((2 * V, V), F32),
            pltpu.VMEM((2 * V, V), F32),
            pltpu.VMEM((2 * V, V), F32),
            pltpu.VMEM((2 * V, V), F32),
            pltpu.SMEM((2, ncol), F32),
            pltpu.SMEM((2, ncol), F32),
            pltpu.SMEM((2, 1, slots), jnp.int32),
            pltpu.SMEM((1, 2), jnp.int32),
            pltpu.SMEM((2, slots, ncol), jnp.int32),
            pltpu.SMEM((2, ncol), jnp.int32),
            pltpu.VMEM((1, V), F32),
            pltpu.SMEM((ncol,), F32),
            pltpu.SemaphoreType.DMA((ITERS, COUNT)),
            pltpu.SemaphoreType.DMA((ITERS, COUNT)),
            pltpu.SemaphoreType.DMA((10,)),
        ],
        compiler_params=pltpu.CompilerParams(
            collective_id=0, has_side_effects=True, vmem_limit_bytes=66000000
        ),
        name="sweeps",
    )(
        amplitudes,
        coulomb,
        inner_list,
        inner_count.T,
        reader_list.transpose(0, 2, 1),
        reader_count,
        virtual_energy.reshape(1, V),
        occupied_energy,
    )


def solution(mesh):
    return jax.shard_map(
        functools.partial(on_device, nrow=mesh.shape["row"], ncol=mesh.shape["col"]),
        mesh=mesh,
        in_specs=(
            P("row", "col", None, None),
            P("row", None, None, None),
            P("row", "col", None),
            P("row", "col"),
            P("row", None, None),
            P("row", None),
            P(),
            P(),
        ),
        out_specs=P("row", "col", None, None),
        check_vma=False,
    )
```

time: 109 us -> 86.2 us (0.79)
  Pallas kernels: 100 us -> 83.1 us
  local copies, waits for them, and re-layouts: 8.23 us -> 1.87 us
    pallas_call x1, Pallas kernels: 100 us -> 83.1 us  [on_device(): pl.pallas_call(functools.partial(kernel, nrow, ncol, slots, V), out_shape...]
    unnamed x15 -> x1, local copies, waits for them, and re-layouts: 8.23 us -> 1.87 us
where the time goes in v2:
time: 86.2 us; the launch traced here: 85 us
  Pallas kernels  83.1 us (96%)
  local copies, waits for them, and re-layouts  1.87 us (2%)
    pallas_call x1, Pallas kernels, on_device(): pl.pallas_call(functools.partial(kernel, nrow, ncol, slots, V), out_shape...  83.1 us
    unnamed x1, local copies, waits for them, and re-layouts  1.87 us

profile of v2, /device:TPU:0, one launch (start us, length us, event | category | flops | bytes accessed | tf_op | source)
XLA Modules:
  0.0 85.0 jit_solution(17370977531985846126)
XLA Ops:
  0.0 83.1 %sweeps.1 = f32[2,1,256,256]{3,2,1,0:T(8,128)} custom-call(f32[2,1,256,256]{3,2,1,0:T(8,128)} %amp_ref.1, bf16[2,16,256,256]{3,2,1,0:T(8,128)(2,1)} %coul_ref.1, s32[2,1,8]{2,1,0:T(1,128)} %ilist_ref.1, s32[1,2]{1,0:T(1,128)} %bitcast.5, s32[2,8,16]{2,1,0:T(8,128)} %bitcast.3, s32[2,16]{1,0:T(2,128)} %rcnt_ref.1, f32[1,256]{1,0:T(1,128)} %bitcast.4, f32[16]{0:T(128)} %occ_ref.1), custom_call_target="tpu_custom_call" | custom-call | tf_op jit(solution)/shard_map/sweeps/pallas_call | solution.py:457
  83.1 1.9 %copy.10 = f32[2,1,256,256]{3,2,1,0:T(8,128)} copy(f32[2,1,256,256]{3,2,1,0:T(8,128)} %sweeps.1) | data formatting | bytes 1048576

commit v3 on v2

--- a/solution.py
+++ b/solution.py
@@ -20,12 +20,12 @@
 L_Q, L_P, L_QB, L_NB, L_NA, L_PB, L_NRB = range(13, 20)
 COL = 20
 N_P, N_Q = 40, 41
-ZR_O, ZR_H, ZR_OA, ZR_HA = range(42, 46)
-ZL_O, ZL_H, ZL_OB, ZL_HB = range(46, 50)
-S_O, S_H, S_M, S_P, S_HM, S_HP, S_2, S_H2 = range(50, 58)
-M_0, M_1, X_0, X_1 = range(58, 62)
-COUNT = 62
-LINEAR_CUT, COUPLED_CUT = 18, 16
+ZR_O, ZR_HP, ZR_HQ, ZR_OA, ZR_HA = range(42, 47)
+ZL_O, ZL_HP, ZL_HQ, ZL_OB, ZL_HB = range(47, 52)
+S_O, S_H, S_M, S_P, S_HM, S_HP, S_2, S_H2A, S_H2B = range(52, 61)
+M_0, M_1, X_0, X_1 = range(61, 65)
+COUNT = 65
+LINEAR_CUT, COUPLED_CUT = 18, 14
 
 
 def kernel(
@@ -64,6 +64,7 @@
     hp, hm, h2 = flip(cp, 2), flip(cm, 2), flip(c2, 2)
     to_y, to_right, to_left = (ry, c), (rp, c), (rm, c)
     to_n, to_zr, to_zl, to_s = (ry, ch), (r, cp), (r, cm), (r, cs)
+    to_zrs, to_zls = (r, flip(cp, 1)), (r, flip(cm, 1))
     nx = nrow // 2
     x, lo = r // 2, lax.rem(r, 2)
     z, hi, core = c // 4, lax.rem(c // 2, 2), lax.rem(c, 2)
@@ -108,7 +109,7 @@
         load.start()
 
     barrier = pltpu.get_barrier_semaphore()
-    for dev in (to_y, to_right, to_left, to_n, to_zr, to_zl, to_s):
+    for dev in (to_y, to_right, to_left, to_n, to_zr, to_zl, to_s, to_zrs, to_zls):
         pl.semaphore_signal(barrier, inc=1, device_id=dev, device_id_type=MESH)
 
     def greet(condition, *devices):
@@ -126,9 +127,9 @@
         greet(jnp.logical_and(opposite, core == 1), place(x + 1, z, lo, hi, a))
     greet(beside, place(x - step, z, lo, hi, core), place(x, z + 2, hi, lo, core))
     for condition, count in (
-        (jnp.logical_or(beside, jnp.logical_and(diagonal, lo != hi)), 11),
-        (jnp.logical_and(diagonal, lo == hi), 10),
-        (opposite, 9),
+        (jnp.logical_or(beside, jnp.logical_and(diagonal, lo != hi)), 13),
+        (jnp.logical_and(diagonal, lo == hi), 12),
+        (opposite, 11),
     ):
         @pl.when(condition)
         def _():
@@ -164,13 +165,17 @@
                     else:
                         acc[at, :] += part
 
-        def open_gather(buf, o):
+        def open_q(buf, o):
             k = cuts[o]
             own = buf.at[s, r]
             send(own.at[k["p"]], o + Y_P, to_y)
             send(own.at[k["q"]], o + R_Q, to_right)
             send(own.at[k["q"]], o + L_Q, to_left)
             send(own.at[k["q"]], o + Y_Q, to_y)
+
+        def open_p(buf, o):
+            k = cuts[o]
+            own = buf.at[s, r]
             send(own.at[k["p"]], o + R_P, to_right)
             send(own.at[k["p"]], o + L_P, to_left)
 
@@ -223,7 +228,8 @@
         start = state[...].astype(BF16)
         amps[s, r] = start
         rows[s, c] = start
-        open_gather(amps, 0)
+        open_q(amps, 0)
+        open_p(amps, 0)
         send(rows.at[s, c], ZR_O, to_zr)
         send(rows.at[s, c], ZL_O, to_zl)
         send(rows.at[s, c], S_O, to_s)
@@ -268,11 +274,13 @@
         relay_q2(amps, 0)
         consume(lin_left, wlin, amps, rp)
         consume(lin_left, wlin, amps, ry)
+        arrived(rows.at[s, ch, lin["p"]], N_P)
+        send(rows.at[s, ch, lin["p"]], ZR_HP, to_zr)
+        send(rows.at[s, ch, lin["p"]], ZL_HP, to_zl)
         relay_nn(amps, 0)
-        arrived(rows.at[s, ch, lin["p"]], N_P)
         arrived(rows.at[s, ch, lin["q"]], N_Q)
-        send(rows.at[s, ch], ZR_H, to_zr)
-        send(rows.at[s, ch], ZL_H, to_zl)
+        send(rows.at[s, ch, lin["q"]], ZR_HQ, to_zr)
+        send(rows.at[s, ch, lin["q"]], ZL_HQ, to_zl)
         send(rows.at[s, ch], S_H, to_s)
         arrived(amps.at[s, ym, lin["q"]], Y_QM)
         consume(lin_left, wlin, amps, ym)
@@ -297,13 +305,15 @@
         def forward(src, key, target, dev):
             message(src, target[0], key, dev, target[1]).start()
 
+        open_q(coups, COL)
+
         @pl.when(opposite)
         def _():
             first = (transit.at[s, 0], X_0)
             forward(block[0], M_0, first, place(x + 1, z, lo, hi, core))
             forward(block[1], M_1, first, place(x - 1, z, lo, hi, core))
 
-        open_gather(coups, COL)
+        open_p(coups, COL)
 
         @pl.when(beside)
         def _():
@@ -327,6 +337,16 @@
             at = slice(a * V, (a + 1) * V)
             linear = coul[c, at, :].astype(F32) + coupling * coups[s, r, at, :].astype(F32)
             base[at, :] = damping * state[at, :] - linear * inv[at, :]
+        arrived(rows.at[s, hm, lin["p"]], ZR_HP)
+        send(rows.at[s, hm, half_a], ZR_HA, to_zr)
+        send(rows.at[s, hm, half_a], S_H2A, to_zrs)
+        arrived(rows.at[s, hp, lin["p"]], ZL_HP)
+        arrived(rows.at[s, hp, lin["q"]], ZL_HQ)
+        send(rows.at[s, hp, half_b], ZL_HB, to_zl)
+        send(rows.at[s, hp, half_b], S_H2B, to_zls)
+        arrived(rows.at[s, hm, lin["q"]], ZR_HQ)
+        send(rows.at[s, hm], S_HM, to_s)
+        send(rows.at[s, hp], S_HP, to_s)
         relay_q(coups, COL)
         relay_n(coups, COL)
 
@@ -343,32 +363,26 @@
                 transit.at[s, 0], X_0, (transit.at[s, 1], X_1), place(x, z + 2, hi, lo, core)
             )
 
-        arrived(rows.at[s, hm], ZR_H)
-        send(rows.at[s, hm, half_a], ZR_HA, to_zr)
-        send(rows.at[s, hm], S_HM, to_s)
-        arrived(rows.at[s, hp], ZL_H)
-        send(rows.at[s, hp, half_b], ZL_HB, to_zl)
-        send(rows.at[s, hp], S_HP, to_s)
         relay_p(coups, COL)
         relay_q2(coups, COL)
-
-        @pl.when(beside)
-        def _():
-            arrived(transit.at[s, 1], X_1)
-            forward(transit.at[s, 1], X_1, final, place(x - step, z, lo, hi, ahead % 3))
-
         arrived(coups.at[s, ry, quad["q"]], COL + Y_Q)
+        for own, key in (
+            (c, S_O), (ch, S_H), (cm, S_M), (cp, S_P), (hm, S_HM), (hp, S_HP), (c2, S_2),
+        ):
+            arrived(rows.at[s, flip(own, 1)], key)
         arrived(rows.at[s, h2, half_a], ZR_HA)
         arrived(rows.at[s, h2, half_b], ZL_HB)
-        send(rows.at[s, h2], S_H2, to_s)
-        for own, key in (
-            (c, S_O), (ch, S_H), (cm, S_M), (cp, S_P),
-            (hm, S_HM), (hp, S_HP), (c2, S_2), (h2, S_H2),
-        ):
-            arrived(rows.at[s, flip(own, 1)], key)
+        arrived(rows.at[s, flip(h2, 1), half_a], S_H2A)
+        arrived(rows.at[s, flip(h2, 1), half_b], S_H2B)
         consume(quad_left, wquad, coups, r, first=True)
         consume(quad_left, wquad, coups, rm)
         relay_nn(coups, COL)
+
+        @pl.when(beside)
+        def _():
+            arrived(transit.at[s, 1], X_1)
+            forward(transit.at[s, 1], X_1, final, place(x - step, z, lo, hi, ahead % 3))
+
         consume(quad_left, wquad, coups, rp)
         consume(quad_left, wquad, coups, ry)
         arrived(coups.at[s, ym, quad["q"]], COL + Y_QM)
@@ -408,9 +422,12 @@
             for key in keys:
                 sizes[o + key] = amps.at[0, r, k[part]]
     sizes[N_P], sizes[N_Q] = amps.at[0, r, lin["p"]], amps.at[0, r, lin["q"]]
-    for key in (ZR_O, ZR_H, ZL_O, ZL_H, *range(S_O, S_H2 + 1)):
+    for part, keys in (("p", (ZR_HP, ZL_HP)), ("q", (ZR_HQ, ZL_HQ))):
+        for key in keys:
+            sizes[key] = rows.at[0, c, lin[part]]
+    for key in (ZR_O, ZL_O, *range(S_O, S_H2A)):
         sizes[key] = rows.at[0, c]
-    for key in (ZR_OA, ZR_HA, ZL_OB, ZL_HB):
+    for key in (ZR_OA, ZR_HA, ZL_OB, ZL_HB, S_H2A, S_H2B):
         sizes[key] = rows.at[0, c, half_a]
 
     def drain(s, carry):
@@ -456,7 +473,7 @@
     vmem = pl.BlockSpec(memory_space=pltpu.VMEM)
     return pl.pallas_call(
         functools.partial(kernel, nrow, ncol, slots, V),
-        out_shape=jax.ShapeDtypeStruct(amplitudes.shape, F32),
+        out_shape=pltpu.VMEM(amplitudes.shape, F32),
         in_specs=[hbm] * 8,
         out_specs=vmem,
         scratch_shapes=[

time: 86.2 us -> 81.3 us (0.943)
  the two profiles are of different devices: /device:TPU:0 before, /device:TPU:54 now
where the time goes in v3:
time: 81.3 us; the launch traced here: 81.2 us
  Pallas kernels  80.4 us (99%)
    pallas_call x1, Pallas kernels, on_device(): pl.pallas_call(functools.partial(kernel, nrow, ncol, slots, V), out_shape...  80.4 us

profile of v3, /device:TPU:54, one launch (start us, length us, event | category | flops | bytes accessed | tf_op | source)
XLA Modules:
  0.0 81.2 jit_solution(13016931016560953972)
XLA Ops:
  0.0 80.4 %sweeps.1 = f32[2,1,256,256]{3,2,1,0:T(8,128)S(1)} custom-call(f32[2,1,256,256]{3,2,1,0:T(8,128)} %amp_ref.1, bf16[2,16,256,256]{3,2,1,0:T(8,128)(2,1)} %coul_ref.1, s32[2,1,8]{2,1,0:T(1,128)} %ilist_ref.1, s32[1,2]{1,0:T(1,128)} %bitcast.5, s32[2,8,16]{2,1,0:T(8,128)} %bitcast.3, s32[2,16]{1,0:T(2,128)} %rcnt_ref.1, f32[1,256]{1,0:T(1,128)} %bitcast.4, ...), custom_call_target="tpu_custom_call" | custom-call | tf_op jit(solution)/shard_map/sweeps/pallas_call | solution.py:474
  80.4 0.8 copy.10

commit v4 on v3

--- a/solution.py
+++ b/solution.py
@@ -365,6 +365,13 @@
 
         relay_p(coups, COL)
         relay_q2(coups, COL)
+
+        @pl.when(beside)
+        def _():
+            arrived(transit.at[s, 1], X_1)
+            forward(transit.at[s, 1], X_1, final, place(x - step, z, lo, hi, ahead % 3))
+
+        relay_nn(coups, COL)
         arrived(coups.at[s, ry, quad["q"]], COL + Y_Q)
         for own, key in (
             (c, S_O), (ch, S_H), (cm, S_M), (cp, S_P), (hm, S_HM), (hp, S_HP), (c2, S_2),
@@ -376,12 +383,6 @@
         arrived(rows.at[s, flip(h2, 1), half_b], S_H2B)
         consume(quad_left, wquad, coups, r, first=True)
         consume(quad_left, wquad, coups, rm)
-        relay_nn(coups, COL)
-
-        @pl.when(beside)
-        def _():
-            arrived(transit.at[s, 1], X_1)
-            forward(transit.at[s, 1], X_1, final, place(x - step, z, lo, hi, ahead % 3))
 
         consume(quad_left, wquad, coups, rp)
         consume(quad_left, wquad, coups, ry)

time: 81.3 us -> 79 us (0.972)
  the two profiles are of different devices: /device:TPU:54 before, /device:TPU:0 now
where the time goes in v4:
time: 79 us; the launch traced here: 78.9 us
  Pallas kernels  78.1 us (99%)
  local copies, waits for them, and re-layouts  0.8 us (1%)
    pallas_call x1, Pallas kernels, on_device(): pl.pallas_call(functools.partial(kernel, nrow, ncol, slots, V), out_shape...  78.1 us

profile of v4, /device:TPU:0, one launch (start us, length us, event | category | flops | bytes accessed | tf_op | source)
XLA Modules:
  0.0 78.9 jit_solution(2554404607765812957)
XLA Ops:
  0.0 78.1 %sweeps.1 = f32[2,1,256,256]{3,2,1,0:T(8,128)S(1)} custom-call(f32[2,1,256,256]{3,2,1,0:T(8,128)} %amp_ref.1, bf16[2,16,256,256]{3,2,1,0:T(8,128)(2,1)} %coul_ref.1, s32[2,1,8]{2,1,0:T(1,128)} %ilist_ref.1, s32[1,2]{1,0:T(1,128)} %bitcast.5, s32[2,8,16]{2,1,0:T(8,128)} %bitcast.3, s32[2,16]{1,0:T(2,128)} %rcnt_ref.1, f32[1,256]{1,0:T(1,128)} %bitcast.4, ...), custom_call_target="tpu_custom_call" | custom-call | tf_op jit(solution)/shard_map/sweeps/pallas_call | solution.py:475
  78.1 0.8 %copy.10 = f32[2,1,256,256]{3,2,1,0:T(8,128)} copy(f32[2,1,256,256]{3,2,1,0:T(8,128)S(1)} %sweeps.1) | data formatting | bytes 1048576

commit v5 on v4

--- a/solution.py
+++ b/solution.py
@@ -305,14 +305,14 @@
         def forward(src, key, target, dev):
             message(src, target[0], key, dev, target[1]).start()
 
-        open_q(coups, COL)
-
         @pl.when(opposite)
         def _():
             first = (transit.at[s, 0], X_0)
             forward(block[0], M_0, first, place(x + 1, z, lo, hi, core))
             forward(block[1], M_1, first, place(x - 1, z, lo, hi, core))
 
+
+        open_q(coups, COL)
         open_p(coups, COL)
 
         @pl.when(beside)
@@ -339,23 +339,12 @@
             base[at, :] = damping * state[at, :] - linear * inv[at, :]
         arrived(rows.at[s, hm, lin["p"]], ZR_HP)
         send(rows.at[s, hm, half_a], ZR_HA, to_zr)
-        send(rows.at[s, hm, half_a], S_H2A, to_zrs)
         arrived(rows.at[s, hp, lin["p"]], ZL_HP)
         arrived(rows.at[s, hp, lin["q"]], ZL_HQ)
         send(rows.at[s, hp, half_b], ZL_HB, to_zl)
-        send(rows.at[s, hp, half_b], S_H2B, to_zls)
         arrived(rows.at[s, hm, lin["q"]], ZR_HQ)
         send(rows.at[s, hm], S_HM, to_s)
         send(rows.at[s, hp], S_HP, to_s)
-        relay_q(coups, COL)
-        relay_n(coups, COL)
-
-        @pl.when(diagonal)
-        def _():
-            for at, px in ((0, x + 1), (1, x - 1)):
-                arrived(transit.at[s, at], X_0 + at)
-                forward(transit.at[s, at], X_0 + at, final, place(px, z, lo, hi, 1))
-
         @pl.when(beside)
         def _():
             arrived(transit.at[s, 0], X_0)
@@ -363,27 +352,35 @@
                 transit.at[s, 0], X_0, (transit.at[s, 1], X_1), place(x, z + 2, hi, lo, core)
             )
 
-        relay_p(coups, COL)
-        relay_q2(coups, COL)
-
+        relay_q(coups, COL)
+        relay_n(coups, COL)
+        @pl.when(diagonal)
+        def _():
+            for at, px in ((0, x + 1), (1, x - 1)):
+                arrived(transit.at[s, at], X_0 + at)
+                forward(transit.at[s, at], X_0 + at, final, place(px, z, lo, hi, 1))
+
+        arrived(rows.at[s, h2, half_a], ZR_HA)
+        send(rows.at[s, h2, half_a], S_H2A, to_s)
         @pl.when(beside)
         def _():
             arrived(transit.at[s, 1], X_1)
             forward(transit.at[s, 1], X_1, final, place(x - step, z, lo, hi, ahead % 3))
 
+        relay_p(coups, COL)
+        arrived(rows.at[s, h2, half_b], ZL_HB)
+        send(rows.at[s, h2, half_b], S_H2B, to_s)
+        relay_q2(coups, COL)
         relay_nn(coups, COL)
         arrived(coups.at[s, ry, quad["q"]], COL + Y_Q)
         for own, key in (
             (c, S_O), (ch, S_H), (cm, S_M), (cp, S_P), (hm, S_HM), (hp, S_HP), (c2, S_2),
         ):
             arrived(rows.at[s, flip(own, 1)], key)
-        arrived(rows.at[s, h2, half_a], ZR_HA)
-        arrived(rows.at[s, h2, half_b], ZL_HB)
         arrived(rows.at[s, flip(h2, 1), half_a], S_H2A)
         arrived(rows.at[s, flip(h2, 1), half_b], S_H2B)
         consume(quad_left, wquad, coups, r, first=True)
         consume(quad_left, wquad, coups, rm)
-
         consume(quad_left, wquad, coups, rp)
         consume(quad_left, wquad, coups, ry)
         arrived(coups.at[s, ym, quad["q"]], COL + Y_QM)

time: 79 us -> 76.5 us (0.968)
  Pallas kernels: 78.1 us -> 75.5 us
    pallas_call x1, Pallas kernels: 78.1 us -> 75.5 us  [on_device(): pl.pallas_call(functools.partial(kernel, nrow, ncol, slots, V), out_shape...]
where the time goes in v5:
time: 76.5 us; the launch traced here: 76.3 us
  Pallas kernels  75.5 us (99%)
  local copies, waits for them, and re-layouts  0.8 us (1%)
    pallas_call x1, Pallas kernels, on_device(): pl.pallas_call(functools.partial(kernel, nrow, ncol, slots, V), out_shape...  75.5 us

profile of v5, /device:TPU:0, one launch (start us, length us, event | category | flops | bytes accessed | tf_op | source)
XLA Modules:
  0.0 76.3 jit_solution(13958398775551575685)
XLA Ops:
  0.0 75.5 %sweeps.1 = f32[2,1,256,256]{3,2,1,0:T(8,128)S(1)} custom-call(f32[2,1,256,256]{3,2,1,0:T(8,128)} %amp_ref.1, bf16[2,16,256,256]{3,2,1,0:T(8,128)(2,1)} %coul_ref.1, s32[2,1,8]{2,1,0:T(1,128)} %ilist_ref.1, s32[1,2]{1,0:T(1,128)} %bitcast.5, s32[2,8,16]{2,1,0:T(8,128)} %bitcast.3, s32[2,16]{1,0:T(2,128)} %rcnt_ref.1, f32[1,256]{1,0:T(1,128)} %bitcast.4, ...), custom_call_target="tpu_custom_call" | custom-call | tf_op jit(solution)/shard_map/sweeps/pallas_call | solution.py:472
  75.5 0.8 %copy.10 = f32[2,1,256,256]{3,2,1,0:T(8,128)} copy(f32[2,1,256,256]{3,2,1,0:T(8,128)S(1)} %sweeps.1) | data formatting | bytes 1048576

commit v6 on v5

--- a/solution.py
+++ b/solution.py
@@ -138,6 +138,46 @@
     for a in range(2):
         loads[a].wait()
 
+    sizes = {}
+    for o, k in cuts.items():
+        for keys, part in (
+            ((Y_P, R_P, L_P), "p"),
+            ((Y_Q, Y_QM, Y_QP, R_Q, L_Q), "q"),
+            ((Y_Q2A, Y_Q2B, R_QA, L_QB), "qa"),
+            ((R_NA, R_NB, R_PA, R_NRA, L_NB, L_NA, L_PB, L_NRB), "pa"),
+        ):
+            for key in keys:
+                sizes[o + key] = amps.at[0, r, k[part]]
+    sizes[N_P], sizes[N_Q] = amps.at[0, r, lin["p"]], amps.at[0, r, lin["q"]]
+    for part, keys in (("p", (ZR_HP, ZL_HP)), ("q", (ZR_HQ, ZL_HQ))):
+        for key in keys:
+            sizes[key] = rows.at[0, c, lin[part]]
+    for key in (ZR_O, ZL_O, *range(S_O, S_H2A)):
+        sizes[key] = rows.at[0, c]
+    for key in (ZR_OA, ZR_HA, ZL_OB, ZL_HB, S_H2A, S_H2B):
+        sizes[key] = rows.at[0, c, half_a]
+
+    def drain(s, carry):
+        def sent(ref, key):
+            pltpu.make_async_remote_copy(
+                src_ref=ref, dst_ref=ref, send_sem=send_sem.at[s, key],
+                recv_sem=recv_sem.at[s, key], device_id=to_y, device_id_type=MESH,
+            ).wait_send()
+
+        for key, ref in sizes.items():
+            sent(ref, key)
+        for a in range(2):
+            @pl.when(jnp.logical_not(mself[a]))
+            def _():
+                sent(mirror.at[0, a], M_0 + a)
+
+        @pl.when(jnp.logical_not(opposite))
+        def _():
+            for a in range(2):
+                sent(transit.at[0, a], X_0 + a)
+
+        return carry
+
     def sweep(s, carry):
         def message(src, dst, key, dev, recv_key=None):
             return pltpu.make_async_remote_copy(
@@ -258,6 +298,11 @@
                 coul_loads[a].wait()
 
         consume(lin_left, wlin, amps, r, first=True)
+
+        @pl.when(s > 0)
+        def _():
+            drain(s - 1, 0)
+
         relay_q(amps, 0)
         relay_n(amps, 0)
         message(amps.at[s, ry, lin["p"]], rows.at[s, c, lin["p"]], N_P, to_n).start()
@@ -270,8 +315,8 @@
         arrived(rows.at[s, cp], ZL_O)
         send(rows.at[s, cp, half_b], ZL_OB, to_zl)
         send(rows.at[s, cp], S_P, to_s)
+        relay_q2(amps, 0)
         consume(lin_left, wlin, amps, rm)
-        relay_q2(amps, 0)
         consume(lin_left, wlin, amps, rp)
         consume(lin_left, wlin, amps, ry)
         arrived(rows.at[s, ch, lin["p"]], N_P)
@@ -409,47 +454,7 @@
     lax.fori_loop(0, ITERS, sweep, 0)
     for a in range(2):
         out_ref[a, 0] = state[a * V:(a + 1) * V, :]
-    sizes = {}
-    for o, k in cuts.items():
-        for keys, part in (
-            ((Y_P, R_P, L_P), "p"),
-            ((Y_Q, Y_QM, Y_QP, R_Q, L_Q), "q"),
-            ((Y_Q2A, Y_Q2B, R_QA, L_QB), "qa"),
-            ((R_NA, R_NB, R_PA, R_NRA, L_NB, L_NA, L_PB, L_NRB), "pa"),
-        ):
-            for key in keys:
-                sizes[o + key] = amps.at[0, r, k[part]]
-    sizes[N_P], sizes[N_Q] = amps.at[0, r, lin["p"]], amps.at[0, r, lin["q"]]
-    for part, keys in (("p", (ZR_HP, ZL_HP)), ("q", (ZR_HQ, ZL_HQ))):
-        for key in keys:
-            sizes[key] = rows.at[0, c, lin[part]]
-    for key in (ZR_O, ZL_O, *range(S_O, S_H2A)):
-        sizes[key] = rows.at[0, c]
-    for key in (ZR_OA, ZR_HA, ZL_OB, ZL_HB, S_H2A, S_H2B):
-        sizes[key] = rows.at[0, c, half_a]
-
-    def drain(s, carry):
-        def sent(ref, key):
-            pltpu.make_async_remote_copy(
-                src_ref=ref, dst_ref=ref, send_sem=send_sem.at[s, key],
-                recv_sem=recv_sem.at[s, key], device_id=to_y, device_id_type=MESH,
-            ).wait_send()
-
-        for key, ref in sizes.items():
-            sent(ref, key)
-        for a in range(2):
-            @pl.when(jnp.logical_not(mself[a]))
-            def _():
-                sent(mirror.at[0, a], M_0 + a)
-
-        @pl.when(jnp.logical_not(opposite))
-        def _():
-            for a in range(2):
-                sent(transit.at[0, a], X_0 + a)
-
-        return carry
-
-    lax.fori_loop(0, ITERS, drain, 0)
+    drain(ITERS - 1, 0)
 
 
 def on_device(

time: 76.5 us -> 76.4 us (level)
  no operation moved by 1% of the time
where the time goes in v6:
time: 76.4 us; the launch traced here: 76.2 us
  Pallas kernels  75.4 us (99%)
  local copies, waits for them, and re-layouts  0.8 us (1%)
    pallas_call x1, Pallas kernels, on_device(): pl.pallas_call(functools.partial(kernel, nrow, ncol, slots, V), out_shape...  75.4 us

profile of v6, /device:TPU:0, one launch (start us, length us, event | category | flops | bytes accessed | tf_op | source)
XLA Modules:
  0.0 76.2 jit_solution(11121619232406309020)
XLA Ops:
  0.0 75.4 %sweeps.1 = f32[2,1,256,256]{3,2,1,0:T(8,128)S(1)} custom-call(f32[2,1,256,256]{3,2,1,0:T(8,128)} %amp_ref.1, bf16[2,16,256,256]{3,2,1,0:T(8,128)(2,1)} %coul_ref.1, s32[2,1,8]{2,1,0:T(1,128)} %ilist_ref.1, s32[1,2]{1,0:T(1,128)} %bitcast.5, s32[2,8,16]{2,1,0:T(8,128)} %bitcast.3, s32[2,16]{1,0:T(2,128)} %rcnt_ref.1, f32[1,256]{1,0:T(1,128)} %bitcast.4, ...), custom_call_target="tpu_custom_call" | custom-call | tf_op jit(solution)/shard_map/sweeps/pallas_call | solution.py:477
  75.4 0.8 %copy.10 = f32[2,1,256,256]{3,2,1,0:T(8,128)} copy(f32[2,1,256,256]{3,2,1,0:T(8,128)S(1)} %sweeps.1) | data formatting | bytes 1048576

commit v7 on v5

--- a/solution.py
+++ b/solution.py
@@ -342,9 +342,6 @@
         arrived(rows.at[s, hp, lin["p"]], ZL_HP)
         arrived(rows.at[s, hp, lin["q"]], ZL_HQ)
         send(rows.at[s, hp, half_b], ZL_HB, to_zl)
-        arrived(rows.at[s, hm, lin["q"]], ZR_HQ)
-        send(rows.at[s, hm], S_HM, to_s)
-        send(rows.at[s, hp], S_HP, to_s)
         @pl.when(beside)
         def _():
             arrived(transit.at[s, 0], X_0)
@@ -353,6 +350,9 @@
             )
 
         relay_q(coups, COL)
+        arrived(rows.at[s, hm, lin["q"]], ZR_HQ)
+        send(rows.at[s, hm], S_HM, to_s)
+        send(rows.at[s, hp], S_HP, to_s)
         relay_n(coups, COL)
         @pl.when(diagonal)
         def _():

time: 76.5 us -> 76.5 us (level)
  no operation moved by 1% of the time
where the time goes in v7:
time: 76.5 us; the launch traced here: 76.3 us
  Pallas kernels  75.5 us (99%)
  local copies, waits for them, and re-layouts  0.8 us (1%)
    pallas_call x1, Pallas kernels, on_device(): pl.pallas_call(functools.partial(kernel, nrow, ncol, slots, V), out_shape...  75.5 us

profile of v7, /device:TPU:0, one launch (start us, length us, event | category | flops | bytes accessed | tf_op | source)
XLA Modules:
  0.0 76.3 jit_solution(17688828253748869625)
XLA Ops:
  0.0 75.5 %sweeps.1 = f32[2,1,256,256]{3,2,1,0:T(8,128)S(1)} custom-call(f32[2,1,256,256]{3,2,1,0:T(8,128)} %amp_ref.1, bf16[2,16,256,256]{3,2,1,0:T(8,128)(2,1)} %coul_ref.1, s32[2,1,8]{2,1,0:T(1,128)} %ilist_ref.1, s32[1,2]{1,0:T(1,128)} %bitcast.5, s32[2,8,16]{2,1,0:T(8,128)} %bitcast.3, s32[2,16]{1,0:T(2,128)} %rcnt_ref.1, f32[1,256]{1,0:T(1,128)} %bitcast.4, ...), custom_call_target="tpu_custom_call" | custom-call | tf_op jit(solution)/shard_map/sweeps/pallas_call | solution.py:472
  75.5 0.8 %copy.10 = f32[2,1,256,256]{3,2,1,0:T(8,128)} copy(f32[2,1,256,256]{3,2,1,0:T(8,128)S(1)} %sweeps.1) | data formatting | bytes 1048576
